TPU v7x, 32 devices: a whole 2x2x4 slice. The times are simulated.
32 devices in a mesh: dp: 4 (over z), rows: 8 (over y, x, core).
Axes of the slice: x: 2, y: 2, z: 4, core: 2. Of those that a mesh axis runs over, the one named last changes fastest.
Arguments:
- inputs: bfloat16 [2, 8192, 9216], P(None, 'dp', 'rows'), may hold values from -21 to 21
- weights: bfloat16 [2, 9216, 4096], P(None, 'rows'), may hold values from -0.0625 to 0.0625
- bias: float32 [2, 4096], P(None, 'rows'), may hold values from -3 to 3
- stitch: float32 [2, 2, 4096], P(None, None, 'rows'), may hold values from 0.2 to 1
- cotangent: bfloat16 [2, 4096, 8192], P(None, 'rows', 'dp'), may hold values from -6 to 6
- valid: int32 [8192], P('dp'), may hold values from 0 to 1, as said below
- size_class: int32 [8192], P('dp'), may hold values from 195 to 227, as said below
Outputs:
- stitched: bfloat16 [2, 4096, 8192], P(None, 'rows', 'dp')
- grad_inputs: bfloat16 [2, 8192, 9216], P(None, 'dp', 'rows')
- grad_weights: float32 [2, 9216, 4096], P(None, 'rows', 'dp')
- grad_bias: float32 [2, 4096], P(None, 'rows')
- grad_stitch: float32 [2, 2, 4096], P(None, None, 'rows')
- rms_values: float32 [3], replicated
Inputs may be any that keep to these rules, and one draw needn't show every extreme that they name: The first image of every aligned block of 2048 images is valid. `size_class`: each entry is 227 or 195.
All inputs are finite; a program needn't handle non-finite values.
Results may differ from a plain program's by a relative error of at most 0.006.
Values may be sent and summed in bfloat16 or wider, within the bound.
A program may use at most 256 MiB of HBM per device.

v0:
```python
import jax
import jax.numpy as jnp
from jax import lax
from jax.sharding import PartitionSpec as P

F = 9216
C = 4096
BLOCK = 128


def chain(own, up):
    size = lax.axis_size("dp")
    here = lax.axis_index("dp")
    got = None
    for step in range(size - 1):
        dest = size - 1 - step + here if up else step - (size - 1) + here
        dest = jnp.clip(dest, 0, size - 1)
        term = lax.dynamic_index_in_dim(own, dest, 0, keepdims=False)
        if got is not None:
            term = (term.astype(jnp.float32) + got.astype(jnp.float32)).astype(jnp.bfloat16)
        pairs = [(z, z + 1) for z in range(step + 1)]
        if not up:
            pairs = [(size - 1 - a, size - 1 - b) for a, b in pairs]
        got = lax.ppermute(term, "dp", pairs)
    return got


def per_device(inputs, weights, bias, stitch, cotangent, valid, size_class):
    rows = lax.axis_size("rows")
    size = lax.axis_size("dp")
    here = lax.axis_index("dp")
    width = inputs.shape[2]
    mine = bias.shape[1]
    step = min(BLOCK, mine)
    blocks = mine // step
    place = lax.iota(jnp.int32, width) % 36
    padded = (place // 6 == 5) | (place % 6 == 5)
    dropped = (size_class == 195)[:, None] & padded[None, :]
    used = jnp.where(dropped[None], jnp.zeros((), jnp.bfloat16), inputs)
    split = weights.reshape(2, width, rows, mine)
    weight_valid = valid.astype(jnp.float32)
    pieces, stitched, grad_bias, grad_stitch, square_pre, square_out = ([], [], [], [], [], [])
    grad_weights = []
    mats = [split[:, :, :, k * step : (k + 1) * step] for k in range(blocks)]
    sums = []
    for k in range(blocks):
        part = jnp.einsum("tfrc,tbf->rctb", mats[k], used, preferred_element_type=jnp.float32)
        sums.append(
            lax.psum_scatter(
                part.reshape(rows * step, 2, -1), "rows", scatter_dimension=0, tiled=True
            )
        )
    for k in range(blocks):
        cut = slice(k * step, (k + 1) * step)
        pre = jnp.transpose(sums[k], (1, 0, 2)) + bias[:, cut, None]
        act = jax.nn.relu(pre)
        mix = stitch[:, :, cut, None]
        out = jnp.sum(mix * act[None], axis=1)
        stitched.append(out.astype(jnp.bfloat16))
        upstream = cotangent[:, cut].astype(jnp.float32) * weight_valid[None, None, :]
        grad_act = jnp.sum(mix * upstream[:, None], axis=0)
        grad_pre = jnp.where(pre > 0, grad_act, 0.0).astype(jnp.bfloat16)
        grad_bias.append(jnp.sum(grad_pre.astype(jnp.float32), axis=2))
        grad_stitch.append(jnp.sum(upstream[:, None] * act[None], axis=3))
        square_pre.append(jnp.sum(weight_valid[None, None, :] * pre * pre))
        square_out.append(jnp.sum(weight_valid[None, None, :] * out * out))
        piece = lax.all_gather(grad_pre, "rows", axis=0)
        pieces.append(piece)
        block = jnp.einsum("tbf,rtcb->rtfc", used, piece, preferred_element_type=jnp.float32)
        block = block.reshape(size, rows // size, 2, width, step)
        own = block.astype(jnp.bfloat16)
        total = lax.dynamic_index_in_dim(block, here, 0, keepdims=False)
        total = total + chain(own, True).astype(jnp.float32) + chain(own, False).astype(jnp.float32)
        grad_weights.append(total)
    total_x = sum(
        (
            jnp.einsum("rtcb,tfrc->tbf", pieces[k], mats[k], preferred_element_type=jnp.float32)
            for k in range(blocks)
        )
    )
    grad_inputs = jnp.where(dropped[None], 0.0, total_x).astype(jnp.bfloat16)
    grad_weights = jnp.stack(grad_weights, axis=0)
    grad_weights = jnp.transpose(grad_weights, (2, 3, 1, 0, 4)).reshape(2, width, -1)
    stitched = jnp.concatenate(stitched, axis=1)
    grad_bias = jnp.concatenate(grad_bias, axis=1)
    grad_stitch = jnp.concatenate(grad_stitch, axis=2)
    used_wide = used.astype(jnp.float32)
    partial_value = jnp.stack(
        [
            jnp.sum(weight_valid[None, :, None] * used_wide * used_wide),
            sum(square_pre),
            sum(square_out),
            jnp.sum(weight_valid),
        ]
    )
    grad_bias, grad_stitch = lax.psum((grad_bias, grad_stitch), "dp")
    totals = lax.psum(partial_value, ("dp", "rows"))
    count = totals[3] / rows
    rms_values = jnp.sqrt(
        jnp.stack(
            [totals[0] / (count * 2 * F), totals[1] / (count * 2 * C), totals[2] / (count * 2 * C)]
        )
    )
    return (stitched, grad_inputs, grad_weights, grad_bias, grad_stitch, rms_values)


def solution(mesh):
    in_specs = (
        P(None, "dp", "rows"),
        P(None, "rows", None),
        P(None, "rows"),
        P(None, None, "rows"),
        P(None, "rows", "dp"),
        P("dp"),
        P("dp"),
    )
    out_specs = (
        P(None, "rows", "dp"),
        P(None, "dp", "rows"),
        P(None, "rows", "dp"),
        P(None, "rows"),
        P(None, None, "rows"),
        P(),
    )
    return jax.shard_map(
        per_device, mesh=mesh, in_specs=in_specs, out_specs=out_specs, check_vma=False
    )
```

profile of v0, /device:TPU:8, one launch (start us, length us, event | category | flops | bytes accessed | tf_op | source)
XLA Modules:
  0.0 1182.2 jit_solution(11360257432043115924)
XLA Ops:
  7.9 24.6 %copy.69 = bf16[2,1152,4096]{1,2,0:T(8,128)(2,1)} copy(bf16[2,1152,4096]{2,1,0:T(8,128)(2,1)} %param.8) | data formatting | bytes 37748736 | tf_op args[1]
  32.6 14.5 %fusion.69 = (bf16[2,1152,8,128]{1,3,2,0:T(8,128)(2,1)}, bf16[2,1152,8,128]{1,3,2,0:T(8,128)(2,1)}, bf16[2,1152,8,128]{1,3,2,0:T(8,128)(2,1)}, bf16[2,1152,8,128]{1,3,2,0:T(8,128)(2,1)}) fusion(bf16[2,1152,8,512]{1,3,2,0:T(8,128)(2,1)} %bitcast.224), kind=kLoop, calls=%fused_computation.159 | loop fusion | bytes 37748736 | tf_op jit(solution)/shard_map/slice | solution.py:44
  48.3 18.3 %convolution_bitcast_fusion.1 = f32[1024,2,2048]{2,0,1:T(8,128)} fusion(bf16[2,1152,1024]{1,2,0:T(8,128)(2,1)} %bitcast.247, bf16[2,2048,1152]{2,1,0:T(8,128)(2,1)} %param.7, pred[2048,1152]{1,0:T(8,128)(4,1)S(1)} %broadcast_and_fusion), kind=kOutput, calls=%fused_computation.25 | convolution fusion | flops 9668395008 | bytes 33292288
  66.7 19.6 %convolution_bitcast_fusion = f32[1024,2,2048]{2,0,1:T(8,128)} fusion(bf16[2,1152,1024]{1,2,0:T(8,128)(2,1)} %bitcast.246, bf16[2,2048,1152]{2,1,0:T(8,128)(2,1)} %param.7, pred[2048,1152]{1,0:T(8,128)(4,1)S(1)} %broadcast_and_fusion), kind=kOutput, calls=%fused_computation.24 | convolution fusion | flops 9668395008 | bytes 33292288
  86.6 20.3 %convolution_bitcast_fusion.2 = f32[1024,2,2048]{2,0,1:T(8,128)} fusion(bf16[2,1152,1024]{1,2,0:T(8,128)(2,1)} %bitcast.248, bf16[2,2048,1152]{2,1,0:T(8,128)(2,1)} %param.7, pred[2048,1152]{1,0:T(8,128)(4,1)S(1)} %broadcast_and_fusion), kind=kOutput, calls=%fused_computation.26 | convolution fusion | flops 9668395008 | bytes 33292288
  106.9 18.3 %convolution_bitcast_fusion.3 = f32[1024,2,2048]{2,0,1:T(8,128)} fusion(bf16[2,1152,1024]{1,2,0:T(8,128)(2,1)} %bitcast.251, bf16[2,2048,1152]{2,1,0:T(8,128)(2,1)} %param.7, pred[2048,1152]{1,0:T(8,128)(4,1)S(1)} %broadcast_and_fusion), kind=kOutput, calls=%fused_computation.27 | convolution fusion | flops 9668395008 | bytes 33292288
  126.0 6.2 convert_multiply_fusion.3
  132.2 51.7 %reduce-scatter.9.cloned.1.call-done = f32[128,2,2048]{2,0,1:T(8,128)} async-done(((f32[1024,2,2048]{2,0,1:T(8,128)}), f32[128,2,2048]{2,0,1:T(8,128)}) %reduce-scatter.9.cloned.1.call-update) | async-done | bytes 2097168 | tf_op jit(solution)/shard_map/reduce_scatter | solution.py:49
  183.9 119.5 %reduce-scatter.11.cloned.1.call-done = f32[128,2,2048]{2,0,1:T(8,128)} async-done(((f32[1024,2,2048]{2,0,1:T(8,128)}), f32[128,2,2048]{2,0,1:T(8,128)}) %reduce-scatter.11.cloned.1.call-update) | async-done | bytes 2097168 | tf_op jit(solution)/shard_map/reduce_scatter | solution.py:49
  303.4 2.7 fusion.56
  306.3 2.4 multiply_reduce_fusion.1
  308.7 3.1 multiply_reduce_fusion
  311.8 111.2 %reduce-scatter.7.cloned.1.call-done = f32[128,2,2048]{2,0,1:T(8,128)} async-done(((f32[1024,2,2048]{2,0,1:T(8,128)}), f32[128,2,2048]{2,0,1:T(8,128)}) %reduce-scatter.7.cloned.1.call-update) | async-done | bytes 2097168 | tf_op jit(solution)/shard_map/reduce_scatter | solution.py:49
  423.0 119.4 %reduce-scatter.5.cloned.1.call-done = f32[128,2,2048]{2,0,1:T(8,128)} async-done(((f32[1024,2,2048]{2,0,1:T(8,128)}), f32[128,2,2048]{2,0,1:T(8,128)}) %reduce-scatter.5.cloned.1.call-update) | async-done | bytes 2097168 | tf_op jit(solution)/shard_map/reduce_scatter | solution.py:49
  542.4 2.7 fusion.54
  550.3 6.0 fusion.49
  558.5 9.4 fusion
  575.0 39.5 %psum.23 = f32[4]{0:T(128)S(1)} all-reduce(f32[4]{0:T(128)S(1)} %pad_maximum_fusion.3), channel_id=1, replica_groups=mesh['dp'=4,'rows'=8] {'dp','rows'}, use_global_device_ids=true, to_apply=%region_32.33 | all-reduce | flops 4 | bytes 32 | tf_op jit(solution)/shard_map/psum | solution.py:97
  618.4 14.8 %all-reduce = (f32[2,512]{1,0:T(2,128)}, f32[2,2,512]{2,1,0:T(2,128)}) all-reduce(f32[2,512]{1,0:T(2,128)S(1)} %pad_maximum_fusion.2, f32[2,2,512]{2,1,0:T(2,128)S(1)} %pad_maximum_fusion.1), channel_id=1, replica_groups=mesh['dp'=4,'rows'=8] {'dp'}, use_global_device_ids=true, to_apply=%region_16.17 | all-reduce | flops 3072 | bytes 24576 | tf_op jit(solution)/shard_map/psum | solution.py:96
  633.9 3.6 pad_maximum_fusion
  637.5 19.4 %fusion.3 = f32[2,8,128,1152]{3,2,1,0:T(8,128)} fusion(bf16[8,2,128,2048]{3,2,1,0:T(8,128)(2,1)} %bitcast.252, bf16[2,2048,1152]{2,1,0:T(8,128)(2,1)} %param.7, pred[2048,1152]{1,0:T(8,128)(4,1)S(1)} %broadcast_and_fusion), kind=kOutput, calls=%fused_computation.8 | convolution fusion | flops 9668395008 | bytes 29622272 | tf_op jit(solution)/shard_map/tbf,rtcb->rtfc/dot_general | solution.py:69
  656.8 4.1 dynamic-slice_bitcast_fusion.1
  664.1 3.3 all-gather.9.cloned.1.call-done
  667.5 18.4 %fusion.9 = f32[2,8,128,1152]{3,2,1,0:T(8,128)} fusion(bf16[8,2,128,2048]{3,2,1,0:T(8,128)(2,1)} %bitcast.254, bf16[2,2048,1152]{2,1,0:T(8,128)(2,1)} %param.7, pred[2048,1152]{1,0:T(8,128)(4,1)S(1)} %broadcast_and_fusion), kind=kOutput, calls=%fused_computation.14 | convolution fusion | flops 9668395008 | bytes 29622272 | tf_op jit(solution)/shard_map/tbf,rtcb->rtfc/dot_general | solution.py:69
  685.9 4.4 convert_element_type.299
  696.1 27.7 %all-gather.11.cloned.1.call-done = bf16[16,128,2048]{2,1,0:T(8,128)(2,1)} async-done(((bf16[2,128,2048]{2,1,0:T(8,128)(2,1)}), bf16[16,128,2048]{2,1,0:T(8,128)(2,1)}) %all-gather.11.cloned.1.call-update) | async-done | bytes 8388624 | tf_op jit(solution)/shard_map/all_gather | solution.py:67
  723.8 18.4 %fusion.7 = f32[2,8,128,1152]{3,2,1,0:T(8,128)} fusion(bf16[8,2,128,2048]{3,2,1,0:T(8,128)(2,1)} %bitcast.258, bf16[2,2048,1152]{2,1,0:T(8,128)(2,1)} %param.7, pred[2048,1152]{1,0:T(8,128)(4,1)S(1)} %broadcast_and_fusion), kind=kOutput, calls=%fused_computation.12 | convolution fusion | flops 9668395008 | bytes 29622272 | tf_op jit(solution)/shard_map/tbf,rtcb->rtfc/dot_general | solution.py:69
  742.1 3.7 dynamic-slice_bitcast_fusion.5
  747.6 18.5 %fusion.20 = f32[2,2048,1152,1]{2,1,0,3:T(8,128)} fusion(bf16[8,2,128,2048]{3,2,1,0:T(8,128)(2,1)} %bitcast.255, bf16[2,1152,8,128]{1,3,2,0:T(8,128)(2,1)} %get-tuple-element.36), kind=kOutput, calls=%fused_computation.33 | convolution fusion | flops 9663676416 | bytes 31981568 | tf_op jit(solution)/shard_map/rtcb,tfrc->tbf/dot_general | solution.py:77
  766.1 17.3 %fusion.18 = f32[2,2048,1152,1]{2,1,0,3:T(8,128)} fusion(bf16[8,2,128,2048]{3,2,1,0:T(8,128)(2,1)} %bitcast.259, bf16[2,1152,8,128]{1,3,2,0:T(8,128)(2,1)S(1)} %bitcast.250), kind=kOutput, calls=%fused_computation.31 | convolution fusion | flops 9663676416 | bytes 31981568 | tf_op jit(solution)/shard_map/rtcb,tfrc->tbf/dot_general | solution.py:77
  783.4 18.8 %fusion.16 = f32[2,2048,1152,1]{2,1,0,3:T(8,128)} fusion(bf16[8,2,128,2048]{3,2,1,0:T(8,128)(2,1)} %bitcast.256, bf16[2,1152,8,128]{1,3,2,0:T(8,128)(2,1)} %get-tuple-element.38), kind=kOutput, calls=%fused_computation.29 | convolution fusion | flops 9663676416 | bytes 31981568 | tf_op jit(solution)/shard_map/rtcb,tfrc->tbf/dot_general | solution.py:77
  802.2 28.0 %fusion.2 = bf16[2,2048,1152]{2,1,0:T(8,128)(2,1)} fusion(f32[2,2048,1152,1]{2,1,0,3:T(8,128)} %fusion.16, f32[2,2048,1152,1]{2,1,0,3:T(8,128)} %fusion.18, f32[2,2048,1152,1]{2,1,0,3:T(8,128)} %fusion.20, bf16[8,2,128,2048]{3,2,1,0:T(8,128)(2,1)} %bitcast.253, pred[2048,1152]{1,0:T(8,128)(4,1)S(1)} %broadcast_and_fusion, ...), kind=kOutput, calls=%fused_computation.4 | convolution fusion | flops 9687269376 | bytes 81526784 | tf_op jit(solution)/shard_map/rtcb,tfrc->tbf/dot_general | solution.py:77
  830.1 18.5 %fusion.5 = f32[2,8,128,1152]{3,2,1,0:T(8,128)} fusion(bf16[8,2,128,2048]{3,2,1,0:T(8,128)(2,1)} %bitcast.257, bf16[2,2048,1152]{2,1,0:T(8,128)(2,1)} %param.7, pred[2048,1152]{1,0:T(8,128)(4,1)S(1)} %broadcast_and_fusion), kind=kOutput, calls=%fused_computation.10 | convolution fusion | flops 9668395008 | bytes 29622272 | tf_op jit(solution)/shard_map/tbf,rtcb->rtfc/dot_general | solution.py:69
  848.7 2.9 dynamic-slice_bitcast_fusion.3
  853.1 2.4 fusion.24
  855.5 3.3 collective-permute-start.19
  858.9 2.4 fusion.32
  865.0 19.2 %collective-permute-done.12 = bf16[2,2,1152,128]{2,3,0,1:T(8,128)(2,1)S(1)} collective-permute-done((bf16[2,2,1152,128]{2,3,0,1:T(8,128)(2,1)S(1)}, bf16[2,2,1152,128]{2,3,0,1:T(8,128)(2,1)S(1)}, u32[]{:S(2)}, u32[]{:S(2)}) %collective-permute-start.12) | collective-permute-done | bytes 1179680 | tf_op jit(solution)/shard_map/ppermute | solution.py:24
  887.3 22.2 %collective-permute-done.19 = bf16[2,2,1152,128]{2,3,0,1:T(8,128)(2,1)S(1)} collective-permute-done((bf16[2,2,1152,128]{2,3,0,1:T(8,128)(2,1)S(1)}, bf16[2,2,1152,128]{2,3,0,1:T(8,128)(2,1)S(1)}, u32[]{:S(2)}, u32[]{:S(2)}) %collective-permute-start.19) | collective-permute-done | bytes 1179680 | tf_op jit(solution)/shard_map/ppermute | solution.py:24
  910.6 1.9 collective-permute-start.7
  912.5 4.6 fusion.25
  917.1 1.9 collective-permute-start.13
  919.0 15.8 %collective-permute-done.1 = bf16[2,2,1152,128]{2,3,0,1:T(8,128)(2,1)S(1)} collective-permute-done((bf16[2,2,1152,128]{2,3,0,1:T(8,128)(2,1)S(1)}, bf16[2,2,1152,128]{2,3,0,1:T(8,128)(2,1)S(1)}, u32[]{:S(2)}, u32[]{:S(2)}) %collective-permute-start.1) | collective-permute-done | bytes 1179680 | tf_op jit(solution)/shard_map/ppermute | solution.py:24
  937.8 3.7 fusion.37
  942.8 17.4 %collective-permute-done.7 = bf16[2,2,1152,128]{2,3,0,1:T(8,128)(2,1)} collective-permute-done((bf16[2,2,1152,128]{2,3,0,1:T(8,128)(2,1)S(1)}, bf16[2,2,1152,128]{2,3,0,1:T(8,128)(2,1)}, u32[]{:S(2)}, u32[]{:S(2)}) %collective-permute-start.7) | collective-permute-done | bytes 1179680 | tf_op jit(solution)/shard_map/ppermute | solution.py:24
  962.2 3.3 fusion.33
  966.7 18.8 %collective-permute-done.13 = bf16[2,2,1152,128]{2,3,0,1:T(8,128)(2,1)} collective-permute-done((bf16[2,2,1152,128]{2,3,0,1:T(8,128)(2,1)S(1)}, bf16[2,2,1152,128]{2,3,0,1:T(8,128)(2,1)}, u32[]{:S(2)}, u32[]{:S(2)}) %collective-permute-start.13) | collective-permute-done | bytes 1179680 | tf_op jit(solution)/shard_map/ppermute | solution.py:24
  986.8 3.4 fusion.29
  991.4 2.0 fusion.23
  993.4 28.3 %collective-permute-done.10 = bf16[2,2,1152,128]{2,3,0,1:T(8,128)(2,1)S(1)} collective-permute-done((bf16[2,2,1152,128]{2,3,0,1:T(8,128)(2,1)}, bf16[2,2,1152,128]{2,3,0,1:T(8,128)(2,1)S(1)}, u32[]{:S(2)}, u32[]{:S(2)}) %collective-permute-start.10) | collective-permute-done | bytes 1179680 | tf_op jit(solution)/shard_map/ppermute | solution.py:24
  1023.9 3.9 collective-permute-start.8
  1028.1 18.9 %collective-permute-done.16 = bf16[2,2,1152,128]{2,3,0,1:T(8,128)(2,1)S(1)} collective-permute-done((bf16[2,2,1152,128]{2,3,0,1:T(8,128)(2,1)}, bf16[2,2,1152,128]{2,3,0,1:T(8,128)(2,1)S(1)}, u32[]{:S(2)}, u32[]{:S(2)}) %collective-permute-start.16) | collective-permute-done | bytes 1179680 | tf_op jit(solution)/shard_map/ppermute | solution.py:24
  1049.3 3.9 collective-permute-start.14
  1053.2 19.1 %collective-permute-done.23 = bf16[2,2,1152,128]{2,3,0,1:T(8,128)(2,1)S(1)} collective-permute-done((bf16[2,2,1152,128]{2,3,0,1:T(8,128)(2,1)S(1)}, bf16[2,2,1152,128]{2,3,0,1:T(8,128)(2,1)S(1)}, u32[]{:S(2)}, u32[]{:S(2)}) %collective-permute-start.23) | collective-permute-done | bytes 1179680 | tf_op jit(solution)/shard_map/ppermute | solution.py:24
  1072.3 2.1 collective-permute-start.11
  1074.4 2.1 fusion.39
  1076.5 1.9 collective-permute-start.17
  1078.4 19.1 %collective-permute-done.5 = bf16[2,2,1152,128]{2,3,0,1:T(8,128)(2,1)S(1)} collective-permute-done((bf16[2,2,1152,128]{2,3,0,1:T(8,128)(2,1)S(1)}, bf16[2,2,1152,128]{2,3,0,1:T(8,128)(2,1)S(1)}, u32[]{:S(2)}, u32[]{:S(2)}) %collective-permute-start.5) | collective-permute-done | bytes 1179680 | tf_op jit(solution)/shard_map/ppermute | solution.py:24
  1097.6 2.1 fusion.45
  1099.7 23.2 %collective-permute-done.11 = bf16[2,2,1152,128]{2,3,0,1:T(8,128)(2,1)S(1)} collective-permute-done((bf16[2,2,1152,128]{2,3,0,1:T(8,128)(2,1)S(1)}, bf16[2,2,1152,128]{2,3,0,1:T(8,128)(2,1)S(1)}, u32[]{:S(2)}, u32[]{:S(2)}) %collective-permute-start.11) | collective-permute-done | bytes 1179680 | tf_op jit(solution)/shard_map/ppermute | solution.py:24
  1123.2 23.3 %collective-permute-done.17 = bf16[2,2,1152,128]{2,3,0,1:T(8,128)(2,1)S(1)} collective-permute-done((bf16[2,2,1152,128]{2,3,0,1:T(8,128)(2,1)S(1)}, bf16[2,2,1152,128]{2,3,0,1:T(8,128)(2,1)S(1)}, u32[]{:S(2)}, u32[]{:S(2)}) %collective-permute-start.17) | collective-permute-done | bytes 1179680 | tf_op jit(solution)/shard_map/ppermute | solution.py:24
  1146.9 4.1 maximum_bitcast_fusion
  1151.0 11.9 %copy.88 = f32[2,1152,2,4,128]{4,3,2,1,0:T(4,128)} copy(f32[2,1152,2,4,128]{1,4,2,0,3:T(8,128)} %maximum_bitcast_fusion) | data formatting | bytes 18874368 | tf_op jit(solution)/shard_map/transpose | solution.py:83
  1162.9 12.2 %reshape.161 = f32[2,1152,1024]{2,1,0:T(8,128)} reshape(f32[2,1152,2,4,128]{4,3,2,1,0:T(4,128)} %copy.88) | data formatting | bytes 18874368 | tf_op jit(solution)/shard_map/reshape | solution.py:83
  (127 shorter events, 49.1 us)
Async XLA Ops:
  7.2 176.7 %reduce-scatter.9.cloned.1.call-start = ((), (), s32[]{:S(2)}) async-start(), calls=%async_computation.6 | async-start | bytes 18874368 | tf_op jit(solution)/shard_map/reduce_scatter | solution.py:49
  66.6 236.8 %reduce-scatter.11.cloned.1.call-start = ((), (), s32[]{:S(2)}) async-start(), calls=%async_computation.7 | async-start | bytes 18874368 | tf_op jit(solution)/shard_map/reduce_scatter | solution.py:49
  86.3 336.6 %reduce-scatter.7.cloned.1.call-start = ((), (), s32[]{:S(2)}) async-start(), calls=%async_computation.5 | async-start | bytes 18874368 | tf_op jit(solution)/shard_map/reduce_scatter | solution.py:49
  106.9 435.6 %reduce-scatter.5.cloned.1.call-start = ((), (), s32[]{:S(2)}) async-start(), calls=%async_computation.4 | async-start | bytes 18874368 | tf_op jit(solution)/shard_map/reduce_scatter | solution.py:49
  125.2 0.7 copy-start.17
  125.2 0.7 copy-start.19
  125.2 0.7 copy-start.18
  125.3 512.2 %all-gather.15.cloned.1.call-start = ((), (), s32[]{:S(2)}) async-start(), calls=%async_computation.11 | async-start | bytes 9437184 | tf_op jit(solution)/shard_map/all_gather | solution.py:67
  303.4 2.9 copy-start.11
  306.3 2.4 copy-start.10
  542.4 2.9 copy-start.9
  542.4 3.9 copy-start.8
  545.3 2.2 copy-start.5
  545.3 2.4 copy-start.6
  545.3 3.0 copy-start.7
  546.3 2.6 copy-start.2
  546.3 3.2 copy-start.3
  546.4 3.8 copy-start.4
  546.4 4.0 copy-start.12
  556.4 111.1 %all-gather.9.cloned.1.call-start = ((), (), s32[]{:S(2)}) async-start(), calls=%async_computation.8 | async-start | bytes 9437184 | tf_op jit(solution)/shard_map/all_gather | solution.py:67
  557.0 166.8 %all-gather.11.cloned.1.call-start = ((), (), s32[]{:S(2)}) async-start(), calls=%async_computation.9 | async-start | bytes 9437184 | tf_op jit(solution)/shard_map/all_gather | solution.py:67
  557.7 225.6 %all-gather.13.cloned.1.call-start = ((), (), s32[]{:S(2)}) async-start(), calls=%async_computation.10 | async-start | bytes 9437184 | tf_op jit(solution)/shard_map/all_gather | solution.py:67
  558.5 75.4 %copy-start.13 = (bf16[2,128,2048]{2,1,0:T(8,128)(2,1)S(1)}, bf16[2,128,2048]{2,1,0:T(8,128)(2,1)}, u32[]{:S(2)}) copy-start(bf16[2,128,2048]{2,1,0:T(8,128)(2,1)} %get-tuple-element.68) | copy-start | bytes 3145732
  661.0 190.6 %collective-permute-start.18 = (bf16[2,2,1152,128]{2,3,0,1:T(8,128)(2,1)}, bf16[2,2,1152,128]{2,3,0,1:T(8,128)(2,1)}, u32[]{:S(2)}, u32[]{:S(2)}) collective-permute-start(bf16[2,2,1152,128]{2,3,0,1:T(8,128)(2,1)} %get-tuple-element.54), channel_id=1, source_target_pairs={{0,8},{1,9},{2,10},{3,11},{4,12},{5,13},{6,14},{7,15}} | collective-permute-start | bytes 3538952 | tf_op jit(solution)/shard_map/ppermute | solution.py:24
  662.2 224.2 %collective-permute-start.21 = (bf16[2,2,1152,128]{2,3,0,1:T(8,128)(2,1)}, bf16[2,2,1152,128]{2,3,0,1:T(8,128)(2,1)}, u32[]{:S(2)}, u32[]{:S(2)}) collective-permute-start(bf16[2,2,1152,128]{2,3,0,1:T(8,128)(2,1)} %get-tuple-element.55), channel_id=1, source_target_pairs={{24,16},{25,17},{26,18},{27,19},{28,20},{29,21},{30,22},{31,23}} | collective-permute-start | bytes 3538952 | tf_op jit(solution)/shard_map/ppermute | solution.py:24
  690.2 2.8 copy-start
  693.1 168.2 %collective-permute-start = (bf16[2,2,1152,128]{2,3,0,1:T(8,128)(2,1)}, bf16[2,2,1152,128]{2,3,0,1:T(8,128)(2,1)}, u32[]{:S(2)}, u32[]{:S(2)}) collective-permute-start(bf16[2,2,1152,128]{2,3,0,1:T(8,128)(2,1)} %get-tuple-element.42), channel_id=1, source_target_pairs={{0,8},{1,9},{2,10},{3,11},{4,12},{5,13},{6,14},{7,15}} | collective-permute-start | bytes 3538952 | tf_op jit(solution)/shard_map/ppermute | solution.py:24
  694.4 222.7 %collective-permute-start.3 = (bf16[2,2,1152,128]{2,3,0,1:T(8,128)(2,1)}, bf16[2,2,1152,128]{2,3,0,1:T(8,128)(2,1)}, u32[]{:S(2)}, u32[]{:S(2)}) collective-permute-start(bf16[2,2,1152,128]{2,3,0,1:T(8,128)(2,1)} %get-tuple-element.43), channel_id=1, source_target_pairs={{24,16},{25,17},{26,18},{27,19},{28,20},{29,21},{30,22},{31,23}} | collective-permute-start | bytes 3538952 | tf_op jit(solution)/shard_map/ppermute | solution.py:24
  745.9 20.2 %slice-start.5 = ((s8[4718592]{0:T(1024)(128)(4,1)}), s8[4194304]{0:T(1024)(128)(4,1)S(1)}, s32[]{:S(2)}) async-start(s8[4718592]{0:T(1024)(128)(4,1)} %bitcast.249), calls=%async_computation.17 | async-start | bytes 8388608
  745.9 20.2 %slice-start.6 = ((s8[4718592]{0:T(1024)(128)(4,1)}), s8[524288]{0:T(1024)(128)(4,1)S(1)}, s32[]{:S(2)}) async-start(s8[4718592]{0:T(1024)(128)(4,1)} %bitcast.249), calls=%async_computation.18 | async-start | bytes 1048576
  745.9 109.7 %collective-permute-start.6 = (bf16[2,2,1152,128]{2,3,0,1:T(8,128)(2,1)}, bf16[2,2,1152,128]{2,3,0,1:T(8,128)(2,1)}, u32[]{:S(2)}, u32[]{:S(2)}) collective-permute-start(bf16[2,2,1152,128]{2,3,0,1:T(8,128)(2,1)} %get-tuple-element.46), channel_id=1, source_target_pairs={{0,8},{1,9},{2,10},{3,11},{4,12},{5,13},{6,14},{7,15}} | collective-permute-start | bytes 3538952 | tf_op jit(solution)/shard_map/ppermute | solution.py:24
  848.7 37.5 %copy-start.1 = (f32[2,8,128,1152]{3,2,1,0:T(8,128)S(1)}, f32[2,8,128,1152]{3,2,1,0:T(8,128)}, u32[]{:S(2)}) copy-start(f32[2,8,128,1152]{3,2,1,0:T(8,128)} %fusion.5) | copy-start | bytes 28311556
  851.6 32.7 %collective-permute-start.12 = (bf16[2,2,1152,128]{2,3,0,1:T(8,128)(2,1)S(1)}, bf16[2,2,1152,128]{2,3,0,1:T(8,128)(2,1)S(1)}, u32[]{:S(2)}, u32[]{:S(2)}) collective-permute-start(bf16[2,2,1152,128]{2,3,0,1:T(8,128)(2,1)S(1)} %get-tuple-element.50), channel_id=1, source_target_pairs={{0,8},{1,9},{2,10},{3,11},{4,12},{5,13},{6,14},{7,15}} | collective-permute-start | bytes 3538952 | tf_op jit(solution)/shard_map/ppermute | solution.py:24
  853.1 109.0 %slice-start.2 = ((s8[9437184]{0:T(1024)(128)(4,1)}), s8[4194304]{0:T(1024)(128)(4,1)S(1)}, s32[]{:S(2)}) async-start(s8[9437184]{0:T(1024)(128)(4,1)} %bitcast.236), calls=%async_computation.14 | async-start | bytes 8388608
  855.5 54.0 %collective-permute-start.19 = (bf16[2,2,1152,128]{2,3,0,1:T(8,128)(2,1)S(1)}, bf16[2,2,1152,128]{2,3,0,1:T(8,128)(2,1)S(1)}, u32[]{:S(2)}, u32[]{:S(2)}) collective-permute-start(bf16[2,2,1152,128]{2,3,0,1:T(8,128)(2,1)S(1)} %fusion.24), channel_id=1, source_target_pairs={{0,8},{8,16},{1,9},{9,17},{2,10},{10,18},{3,11},{11,19},{4,12},{12... | collective-permute-start | bytes 3538952 | tf_op jit(solution)/shard_map/ppermute | solution.py:24
  858.9 78.9 %slice-start = ((s8[4718592]{0:T(1024)(128)(4,1)}), s8[4194304]{0:T(1024)(128)(4,1)S(1)}, s32[]{:S(2)}) async-start(s8[4718592]{0:T(1024)(128)(4,1)} %bitcast.225), calls=%async_computation.12 | async-start | bytes 8388608
  861.3 100.9 %slice-start.3 = ((s8[9437184]{0:T(1024)(128)(4,1)}), s8[4194304]{0:T(1024)(128)(4,1)S(1)}, s32[]{:S(2)}) async-start(s8[9437184]{0:T(1024)(128)(4,1)} %bitcast.236), calls=%async_computation.15 | async-start | bytes 8388608
  861.3 80.3 %collective-permute-start.9 = (bf16[2,2,1152,128]{2,3,0,1:T(8,128)(2,1)S(1)}, bf16[2,2,1152,128]{2,3,0,1:T(8,128)(2,1)}, u32[]{:S(2)}, u32[]{:S(2)}) collective-permute-start(bf16[2,2,1152,128]{2,3,0,1:T(8,128)(2,1)S(1)} %get-tuple-element.47), channel_id=1, source_target_pairs={{24,16},{25,17},{26,18},{27,19},{28,20},{29,21},{30,22},{31,23}} | collective-permute-start | bytes 3538952 | tf_op jit(solution)/shard_map/ppermute | solution.py:24
  865.0 72.8 %slice-start.1 = ((s8[4718592]{0:T(1024)(128)(4,1)}), s8[524288]{0:T(1024)(128)(4,1)S(1)}, s32[]{:S(2)}) async-start(s8[4718592]{0:T(1024)(128)(4,1)} %bitcast.225), calls=%async_computation.13 | async-start | bytes 1048576
  884.3 50.6 %collective-permute-start.1 = (bf16[2,2,1152,128]{2,3,0,1:T(8,128)(2,1)S(1)}, bf16[2,2,1152,128]{2,3,0,1:T(8,128)(2,1)S(1)}, u32[]{:S(2)}, u32[]{:S(2)}) collective-permute-start(bf16[2,2,1152,128]{2,3,0,1:T(8,128)(2,1)S(1)} %fusion.36), channel_id=1, source_target_pairs={{0,8},{8,16},{1,9},{9,17},{2,10},{10,18},{3,11},{11,19},{4,12},{12... | collective-permute-start | bytes 3538952 | tf_op jit(solution)/shard_map/ppermute | solution.py:24
  886.5 75.7 %slice-start.4 = ((s8[9437184]{0:T(1024)(128)(4,1)}), s8[1048576]{0:T(1024)(128)(4,1)S(1)}, s32[]{:S(2)}) async-start(s8[9437184]{0:T(1024)(128)(4,1)} %bitcast.236), calls=%async_computation.16 | async-start | bytes 2097152
  886.5 79.0 %collective-permute-start.15 = (bf16[2,2,1152,128]{2,3,0,1:T(8,128)(2,1)S(1)}, bf16[2,2,1152,128]{2,3,0,1:T(8,128)(2,1)S(1)}, u32[]{:S(2)}, u32[]{:S(2)}) collective-permute-start(bf16[2,2,1152,128]{2,3,0,1:T(8,128)(2,1)S(1)} %get-tuple-element.51), channel_id=1, source_target_pairs={{24,16},{25,17},{26,18},{27,19},{28,20},{29,21},{30,22},{31,23}} | collective-permute-start | bytes 3538952 | tf_op jit(solution)/shard_map/ppermute | solution.py:24
  909.6 1.0 copy-start.15
  910.6 49.6 %collective-permute-start.7 = (bf16[2,2,1152,128]{2,3,0,1:T(8,128)(2,1)S(1)}, bf16[2,2,1152,128]{2,3,0,1:T(8,128)(2,1)}, u32[]{:S(2)}, u32[]{:S(2)}) collective-permute-start(bf16[2,2,1152,128]{2,3,0,1:T(8,128)(2,1)S(1)} %fusion.32), channel_id=1, source_target_pairs={{0,8},{8,16},{1,9},{9,17},{2,10},{10,18},{3,11},{11,19},{4,12},{12... | collective-permute-start | bytes 3538952 | tf_op jit(solution)/shard_map/ppermute | solution.py:24
  917.1 68.4 %collective-permute-start.13 = (bf16[2,2,1152,128]{2,3,0,1:T(8,128)(2,1)S(1)}, bf16[2,2,1152,128]{2,3,0,1:T(8,128)(2,1)}, u32[]{:S(2)}, u32[]{:S(2)}) collective-permute-start(bf16[2,2,1152,128]{2,3,0,1:T(8,128)(2,1)S(1)} %fusion.28), channel_id=1, source_target_pairs={{0,8},{8,16},{1,9},{9,17},{2,10},{10,18},{3,11},{11,19},{4,12},{12... | collective-permute-start | bytes 3538952 | tf_op jit(solution)/shard_map/ppermute | solution.py:24
  934.8 1.1 copy-start.16
  935.9 113.4 %collective-permute-start.20 = (bf16[2,2,1152,128]{2,3,0,1:T(8,128)(2,1)S(1)}, bf16[2,2,1152,128]{2,3,0,1:T(8,128)(2,1)S(1)}, u32[]{:S(2)}, u32[]{:S(2)}) collective-permute-start(bf16[2,2,1152,128]{2,3,0,1:T(8,128)(2,1)S(1)} %get-tuple-element.52), channel_id=1, source_target_pairs={{0,8},{8,16},{16,24},{1,9},{9,17},{17,25},{2,10},{10,18},{18,26},{... | collective-permute-start | bytes 3538952 | tf_op jit(solution)/shard_map/ppermute | solution.py:24
  941.6 48.6 %collective-permute-start.22 = (bf16[2,2,1152,128]{2,3,0,1:T(8,128)(2,1)}, bf16[2,2,1152,128]{2,3,0,1:T(8,128)(2,1)S(1)}, u32[]{:S(2)}, u32[]{:S(2)}) collective-permute-start(bf16[2,2,1152,128]{2,3,0,1:T(8,128)(2,1)} %get-tuple-element.53), channel_id=1, source_target_pairs={{24,16},{16,8},{25,17},{17,9},{26,18},{18,10},{27,19},{19,11},{28,... | collective-permute-start | bytes 3538952 | tf_op jit(solution)/shard_map/ppermute | solution.py:24
  960.2 116.3 %collective-permute-start.2 = (bf16[2,2,1152,128]{2,3,0,1:T(8,128)(2,1)}, bf16[2,2,1152,128]{2,3,0,1:T(8,128)(2,1)S(1)}, u32[]{:S(2)}, u32[]{:S(2)}) collective-permute-start(bf16[2,2,1152,128]{2,3,0,1:T(8,128)(2,1)} %get-tuple-element.40), channel_id=1, source_target_pairs={{0,8},{8,16},{16,24},{1,9},{9,17},{17,25},{2,10},{10,18},{18,26},{... | collective-permute-start | bytes 3538952 | tf_op jit(solution)/shard_map/ppermute | solution.py:24
  965.5 58.4 %collective-permute-start.4 = (bf16[2,2,1152,128]{2,3,0,1:T(8,128)(2,1)}, bf16[2,2,1152,128]{2,3,0,1:T(8,128)(2,1)S(1)}, u32[]{:S(2)}, u32[]{:S(2)}) collective-permute-start(bf16[2,2,1152,128]{2,3,0,1:T(8,128)(2,1)} %get-tuple-element.41), channel_id=1, source_target_pairs={{24,16},{16,8},{25,17},{17,9},{26,18},{18,10},{27,19},{19,11},{28,... | collective-permute-start | bytes 3538952 | tf_op jit(solution)/shard_map/ppermute | solution.py:24
  985.5 36.2 %collective-permute-start.10 = (bf16[2,2,1152,128]{2,3,0,1:T(8,128)(2,1)}, bf16[2,2,1152,128]{2,3,0,1:T(8,128)(2,1)S(1)}, u32[]{:S(2)}, u32[]{:S(2)}) collective-permute-start(bf16[2,2,1152,128]{2,3,0,1:T(8,128)(2,1)} %get-tuple-element.45), channel_id=1, source_target_pairs={{24,16},{16,8},{25,17},{17,9},{26,18},{18,10},{27,19},{19,11},{28,... | collective-permute-start | bytes 3538952 | tf_op jit(solution)/shard_map/ppermute | solution.py:24
  990.2 56.9 %collective-permute-start.16 = (bf16[2,2,1152,128]{2,3,0,1:T(8,128)(2,1)}, bf16[2,2,1152,128]{2,3,0,1:T(8,128)(2,1)S(1)}, u32[]{:S(2)}, u32[]{:S(2)}) collective-permute-start(bf16[2,2,1152,128]{2,3,0,1:T(8,128)(2,1)} %get-tuple-element.49), channel_id=1, source_target_pairs={{24,16},{16,8},{25,17},{17,9},{26,18},{18,10},{27,19},{19,11},{28,... | collective-permute-start | bytes 3538952 | tf_op jit(solution)/shard_map/ppermute | solution.py:24
  1021.7 50.6 %collective-permute-start.23 = (bf16[2,2,1152,128]{2,3,0,1:T(8,128)(2,1)S(1)}, bf16[2,2,1152,128]{2,3,0,1:T(8,128)(2,1)S(1)}, u32[]{:S(2)}, u32[]{:S(2)}) collective-permute-start(bf16[2,2,1152,128]{2,3,0,1:T(8,128)(2,1)S(1)} %fusion.23), channel_id=1, source_target_pairs={{24,16},{16,8},{8,0},{25,17},{17,9},{9,1},{26,18},{18,10},{10,2},{... | collective-permute-start | bytes 3538952 | tf_op jit(solution)/shard_map/ppermute | solution.py:24
  1023.9 75.7 %collective-permute-start.8 = (bf16[2,2,1152,128]{2,3,0,1:T(8,128)(2,1)S(1)}, bf16[2,2,1152,128]{2,3,0,1:T(8,128)(2,1)S(1)}, u32[]{:S(2)}, u32[]{:S(2)}) collective-permute-start(bf16[2,2,1152,128]{2,3,0,1:T(8,128)(2,1)S(1)} %get-tuple-element.44), channel_id=1, source_target_pairs={{0,8},{8,16},{16,24},{1,9},{9,17},{17,25},{2,10},{10,18},{18,26},{... | collective-permute-start | bytes 3538952 | tf_op jit(solution)/shard_map/ppermute | solution.py:24
  1028.1 21.1 %copy-start.14 = (bf16[2,2,1152,128]{2,3,0,1:T(8,128)(2,1)S(1)}, bf16[2,2,1152,128]{2,3,0,1:T(8,128)(2,1)}, u32[]{:S(2)}) copy-start(bf16[2,2,1152,128]{2,3,0,1:T(8,128)(2,1)} %get-tuple-element.48) | copy-start | bytes 3538948
  1047.0 50.6 %collective-permute-start.5 = (bf16[2,2,1152,128]{2,3,0,1:T(8,128)(2,1)S(1)}, bf16[2,2,1152,128]{2,3,0,1:T(8,128)(2,1)S(1)}, u32[]{:S(2)}, u32[]{:S(2)}) collective-permute-start(bf16[2,2,1152,128]{2,3,0,1:T(8,128)(2,1)S(1)} %fusion.35), channel_id=1, source_target_pairs={{24,16},{16,8},{8,0},{25,17},{17,9},{9,1},{26,18},{18,10},{10,2},{... | collective-permute-start | bytes 3538952 | tf_op jit(solution)/shard_map/ppermute | solution.py:24
  1049.3 74.0 %collective-permute-start.14 = (bf16[2,2,1152,128]{2,3,0,1:T(8,128)(2,1)S(1)}, bf16[2,2,1152,128]{2,3,0,1:T(8,128)(2,1)S(1)}, u32[]{:S(2)}, u32[]{:S(2)}) collective-permute-start(bf16[2,2,1152,128]{2,3,0,1:T(8,128)(2,1)S(1)} %copy-done.14), channel_id=1, source_target_pairs={{0,8},{8,16},{16,24},{1,9},{9,17},{17,25},{2,10},{10,18},{18,26},{... | collective-permute-start | bytes 3538952 | tf_op jit(solution)/shard_map/ppermute | solution.py:24
  1072.3 50.6 %collective-permute-start.11 = (bf16[2,2,1152,128]{2,3,0,1:T(8,128)(2,1)S(1)}, bf16[2,2,1152,128]{2,3,0,1:T(8,128)(2,1)S(1)}, u32[]{:S(2)}, u32[]{:S(2)}) collective-permute-start(bf16[2,2,1152,128]{2,3,0,1:T(8,128)(2,1)S(1)} %fusion.31), channel_id=1, source_target_pairs={{24,16},{16,8},{8,0},{25,17},{17,9},{9,1},{26,18},{18,10},{10,2},{... | collective-permute-start | bytes 3538952 | tf_op jit(solution)/shard_map/ppermute | solution.py:24
  1076.5 70.0 %collective-permute-start.17 = (bf16[2,2,1152,128]{2,3,0,1:T(8,128)(2,1)S(1)}, bf16[2,2,1152,128]{2,3,0,1:T(8,128)(2,1)S(1)}, u32[]{:S(2)}, u32[]{:S(2)}) collective-permute-start(bf16[2,2,1152,128]{2,3,0,1:T(8,128)(2,1)S(1)} %fusion.27), channel_id=1, source_target_pairs={{24,16},{16,8},{8,0},{25,17},{17,9},{9,1},{26,18},{18,10},{10,2},{... | collective-permute-start | bytes 3538952 | tf_op jit(solution)/shard_map/ppermute | solution.py:24
Sparse Core Ops, SparseCore 0:
  66.8 117.1 reduce-scatter.8
  187.5 115.9 reduce-scatter.10
  307.0 115.9 reduce-scatter.6
  426.4 115.9 reduce-scatter.4
  556.5 54.6 all-gather.14
  613.0 54.4 all-gather.8
  669.3 54.3 all-gather.10
  725.7 54.3 all-gather.12
where the time goes:
time: 1190 us; the launch traced here: 1180 us
  waiting for transfers between devices  660 us (55%)
  matrix products  234 us (20%)
  local copies, waits for them, and re-layouts  83.1 us (7%)
  other arithmetic  80.9 us (7%)
  blocking collectives  54.4 us (5%)
  starting transfers between devices  46.9 us (4%)
  between operations  23.4 us (2%)
    reduce_scatter x4, waiting for transfers between devices, per_device(): lax.psum_scatter(part.reshape(rows * step, 2, -1), 'rows', scatter_dimens...  402 us
    ppermute x24, waiting for transfers between devices, chain(): got = lax.ppermute(term, 'dp', pairs)  225 us
    dot_general x4, matrix products, per_device(): jnp.einsum('rtcb,tfrc->tbf', pieces[k], mats[k], preferred_element_type=j...  82.5 us
    unnamed x4, matrix products  76.5 us
    dot_general x4, matrix products, per_device(): jnp.einsum('tbf,rtcb->rtfc', used, piece, preferred_element_type=jnp.floa...  74.6 us
    ppermute x24, starting transfers between devices, chain(): got = lax.ppermute(term, 'dp', pairs)  45.8 us
    psum x1, blocking collectives, per_device(): totals = lax.psum(partial_value, ('dp', 'rows'))  39.5 us
    unnamed x55, local copies, waits for them, and re-layouts  31.3 us
  transfers between devices with their start and end apart: 32, of which 17 were waited for; matrix products, arithmetic and copies ran while one was open for 25% of the time, Pallas kernels for 0%

commit v1 on v0

--- a/solution.py
+++ b/solution.py
@@ -94,7 +94,9 @@
         ]
     )
     grad_bias, grad_stitch = lax.psum((grad_bias, grad_stitch), "dp")
-    totals = lax.psum(partial_value, ("dp", "rows"))
+    totals = partial_value
+    for axis in ("rows", "dp"):
+        totals = lax.psum(totals, axis)
     count = totals[3] / rows
     rms_values = jnp.sqrt(
         jnp.stack(

time: 1190 us -> 1190 us (level)
  waiting for transfers between devices: 660 us -> 686 us
  blocking collectives: 54.4 us -> 28.5 us
    psum x1, blocking collectives: 39.5 us -> 12.8 us  [per_device(): totals = lax.psum(totals, axis)]
    all_gather x4, waiting for transfers between devices: 31 us -> 57.4 us  [per_device(): piece = lax.all_gather(grad_pre, 'rows', axis=0)]
where the time goes in v1:
time: 1190 us; the launch traced here: 1180 us
  waiting for transfers between devices  686 us (58%)
  matrix products  233 us (20%)
  local copies, waits for them, and re-layouts  83.1 us (7%)
  other arithmetic  80.9 us (7%)
  starting transfers between devices  46.9 us (4%)
  blocking collectives  28.5 us (2%)
  between operations  23.3 us (2%)
    reduce_scatter x4, waiting for transfers between devices, per_device(): lax.psum_scatter(part.reshape(rows * step, 2, -1), 'rows', scatter_dimens...  402 us
    ppermute x24, waiting for transfers between devices, chain(): got = lax.ppermute(term, 'dp', pairs)  225 us
    dot_general x4, matrix products, per_device(): jnp.einsum('rtcb,tfrc->tbf', pieces[k], mats[k], preferred_element_type=j...  82.5 us
    unnamed x4, matrix products  76.5 us
    dot_general x4, matrix products, per_device(): jnp.einsum('tbf,rtcb->rtfc', used, piece, preferred_element_type=jnp.floa...  73.7 us
    all_gather x4, waiting for transfers between devices, per_device(): piece = lax.all_gather(grad_pre, 'rows', axis=0)  57.4 us
    ppermute x24, starting transfers between devices, chain(): got = lax.ppermute(term, 'dp', pairs)  45.8 us
    unnamed x55, local copies, waits for them, and re-layouts  31.3 us
  transfers between devices with their start and end apart: 32, of which 17 were waited for; matrix products, arithmetic and copies ran while one was open for 25% of the time, Pallas kernels for 0%

profile of v1, /device:TPU:8, one launch (start us, length us, event | category | flops | bytes accessed | tf_op | source)
XLA Modules:
  0.0 1181.8 jit_solution(7154522752120335670)
XLA Ops:
  7.9 24.6 %copy.69 = bf16[2,1152,4096]{1,2,0:T(8,128)(2,1)} copy(bf16[2,1152,4096]{2,1,0:T(8,128)(2,1)} %param.8) | data formatting | bytes 37748736 | tf_op args[1]
  32.6 14.5 %fusion.69 = (bf16[2,1152,8,128]{1,3,2,0:T(8,128)(2,1)}, bf16[2,1152,8,128]{1,3,2,0:T(8,128)(2,1)}, bf16[2,1152,8,128]{1,3,2,0:T(8,128)(2,1)}, bf16[2,1152,8,128]{1,3,2,0:T(8,128)(2,1)}) fusion(bf16[2,1152,8,512]{1,3,2,0:T(8,128)(2,1)} %bitcast.224), kind=kLoop, calls=%fused_computation.159 | loop fusion | bytes 37748736 | tf_op jit(solution)/shard_map/slice | solution.py:44
  48.3 18.3 %convolution_bitcast_fusion.1 = f32[1024,2,2048]{2,0,1:T(8,128)} fusion(bf16[2,1152,1024]{1,2,0:T(8,128)(2,1)} %bitcast.247, bf16[2,2048,1152]{2,1,0:T(8,128)(2,1)} %param.7, pred[2048,1152]{1,0:T(8,128)(4,1)S(1)} %broadcast_and_fusion), kind=kOutput, calls=%fused_computation.25 | convolution fusion | flops 9668395008 | bytes 33292288
  66.7 19.6 %convolution_bitcast_fusion = f32[1024,2,2048]{2,0,1:T(8,128)} fusion(bf16[2,1152,1024]{1,2,0:T(8,128)(2,1)} %bitcast.246, bf16[2,2048,1152]{2,1,0:T(8,128)(2,1)} %param.7, pred[2048,1152]{1,0:T(8,128)(4,1)S(1)} %broadcast_and_fusion), kind=kOutput, calls=%fused_computation.24 | convolution fusion | flops 9668395008 | bytes 33292288
  86.6 20.3 %convolution_bitcast_fusion.2 = f32[1024,2,2048]{2,0,1:T(8,128)} fusion(bf16[2,1152,1024]{1,2,0:T(8,128)(2,1)} %bitcast.248, bf16[2,2048,1152]{2,1,0:T(8,128)(2,1)} %param.7, pred[2048,1152]{1,0:T(8,128)(4,1)S(1)} %broadcast_and_fusion), kind=kOutput, calls=%fused_computation.26 | convolution fusion | flops 9668395008 | bytes 33292288
  106.9 18.3 %convolution_bitcast_fusion.3 = f32[1024,2,2048]{2,0,1:T(8,128)} fusion(bf16[2,1152,1024]{1,2,0:T(8,128)(2,1)} %bitcast.251, bf16[2,2048,1152]{2,1,0:T(8,128)(2,1)} %param.7, pred[2048,1152]{1,0:T(8,128)(4,1)S(1)} %broadcast_and_fusion), kind=kOutput, calls=%fused_computation.27 | convolution fusion | flops 9668395008 | bytes 33292288
  126.0 6.2 convert_multiply_fusion.3
  132.2 51.7 %reduce-scatter.9.cloned.1.call-done = f32[128,2,2048]{2,0,1:T(8,128)} async-done(((f32[1024,2,2048]{2,0,1:T(8,128)}), f32[128,2,2048]{2,0,1:T(8,128)}) %reduce-scatter.9.cloned.1.call-update) | async-done | bytes 2097168 | tf_op jit(solution)/shard_map/reduce_scatter | solution.py:49
  183.9 119.5 %reduce-scatter.11.cloned.1.call-done = f32[128,2,2048]{2,0,1:T(8,128)} async-done(((f32[1024,2,2048]{2,0,1:T(8,128)}), f32[128,2,2048]{2,0,1:T(8,128)}) %reduce-scatter.11.cloned.1.call-update) | async-done | bytes 2097168 | tf_op jit(solution)/shard_map/reduce_scatter | solution.py:49
  303.4 2.7 fusion.56
  306.3 2.4 multiply_reduce_fusion.1
  308.7 3.1 multiply_reduce_fusion
  311.8 111.2 %reduce-scatter.7.cloned.1.call-done = f32[128,2,2048]{2,0,1:T(8,128)} async-done(((f32[1024,2,2048]{2,0,1:T(8,128)}), f32[128,2,2048]{2,0,1:T(8,128)}) %reduce-scatter.7.cloned.1.call-update) | async-done | bytes 2097168 | tf_op jit(solution)/shard_map/reduce_scatter | solution.py:49
  423.0 119.4 %reduce-scatter.5.cloned.1.call-done = f32[128,2,2048]{2,0,1:T(8,128)} async-done(((f32[1024,2,2048]{2,0,1:T(8,128)}), f32[128,2,2048]{2,0,1:T(8,128)}) %reduce-scatter.5.cloned.1.call-update) | async-done | bytes 2097168 | tf_op jit(solution)/shard_map/reduce_scatter | solution.py:49
  542.4 2.7 fusion.54
  550.3 6.0 fusion.49
  558.5 9.4 fusion
  575.0 12.8 %psum.30 = f32[4]{0:T(128)S(1)} all-reduce(f32[4]{0:T(128)S(1)} %pad_maximum_fusion.3), channel_id=1, replica_groups=mesh['dp'=4,'rows'=8] {'rows'}, use_global_device_ids=true, to_apply=%region_32.33 | all-reduce | flops 4 | bytes 32 | tf_op jit(solution)/shard_map/psum | solution.py:99
  587.8 15.8 %all-reduce = (f32[2,512]{1,0:T(2,128)}, f32[2,2,512]{2,1,0:T(2,128)}, f32[4]{0:T(128)S(1)}) all-reduce(f32[2,512]{1,0:T(2,128)S(1)} %pad_maximum_fusion.2, f32[2,2,512]{2,1,0:T(2,128)S(1)} %pad_maximum_fusion.1, f32[4]{0:T(128)S(1)} %psum.30), channel_id=1, replica_groups=mesh['dp'=4,'rows'=8] {'dp'}, use_global_device_ids=true, to_apply=%region_16.17 | all-reduce | flops 3076 | bytes 24608 | tf_op jit(solution)/shard_map/psum | solution.py:96
  608.0 3.6 pad_maximum_fusion
  611.6 18.4 %fusion.3 = f32[2,8,128,1152]{3,2,1,0:T(8,128)} fusion(bf16[8,2,128,2048]{3,2,1,0:T(8,128)(2,1)} %bitcast.252, bf16[2,2048,1152]{2,1,0:T(8,128)(2,1)} %param.7, pred[2048,1152]{1,0:T(8,128)(4,1)S(1)} %broadcast_and_fusion), kind=kOutput, calls=%fused_computation.8 | convolution fusion | flops 9668395008 | bytes 29622272 | tf_op jit(solution)/shard_map/tbf,rtcb->rtfc/dot_general | solution.py:69
  630.1 4.1 dynamic-slice_bitcast_fusion.1
  637.3 29.7 %all-gather.9.cloned.1.call-done = bf16[16,128,2048]{2,1,0:T(8,128)(2,1)} async-done(((bf16[2,128,2048]{2,1,0:T(8,128)(2,1)}), bf16[16,128,2048]{2,1,0:T(8,128)(2,1)}) %all-gather.9.cloned.1.call-update) | async-done | bytes 8388624 | tf_op jit(solution)/shard_map/all_gather | solution.py:67
  667.1 18.4 %fusion.9 = f32[2,8,128,1152]{3,2,1,0:T(8,128)} fusion(bf16[8,2,128,2048]{3,2,1,0:T(8,128)(2,1)} %bitcast.254, bf16[2,2048,1152]{2,1,0:T(8,128)(2,1)} %param.7, pred[2048,1152]{1,0:T(8,128)(4,1)S(1)} %broadcast_and_fusion), kind=kOutput, calls=%fused_computation.14 | convolution fusion | flops 9668395008 | bytes 29622272 | tf_op jit(solution)/shard_map/tbf,rtcb->rtfc/dot_general | solution.py:69
  685.5 4.4 convert_element_type.299
  695.7 27.7 %all-gather.11.cloned.1.call-done = bf16[16,128,2048]{2,1,0:T(8,128)(2,1)} async-done(((bf16[2,128,2048]{2,1,0:T(8,128)(2,1)}), bf16[16,128,2048]{2,1,0:T(8,128)(2,1)}) %all-gather.11.cloned.1.call-update) | async-done | bytes 8388624 | tf_op jit(solution)/shard_map/all_gather | solution.py:67
  723.4 18.4 %fusion.7 = f32[2,8,128,1152]{3,2,1,0:T(8,128)} fusion(bf16[8,2,128,2048]{3,2,1,0:T(8,128)(2,1)} %bitcast.258, bf16[2,2048,1152]{2,1,0:T(8,128)(2,1)} %param.7, pred[2048,1152]{1,0:T(8,128)(4,1)S(1)} %broadcast_and_fusion), kind=kOutput, calls=%fused_computation.12 | convolution fusion | flops 9668395008 | bytes 29622272 | tf_op jit(solution)/shard_map/tbf,rtcb->rtfc/dot_general | solution.py:69
  741.7 3.7 dynamic-slice_bitcast_fusion.5
  747.2 18.5 %fusion.20 = f32[2,2048,1152,1]{2,1,0,3:T(8,128)} fusion(bf16[8,2,128,2048]{3,2,1,0:T(8,128)(2,1)} %bitcast.255, bf16[2,1152,8,128]{1,3,2,0:T(8,128)(2,1)} %get-tuple-element.37), kind=kOutput, calls=%fused_computation.33 | convolution fusion | flops 9663676416 | bytes 31981568 | tf_op jit(solution)/shard_map/rtcb,tfrc->tbf/dot_general | solution.py:77
  765.7 17.2 %fusion.18 = f32[2,2048,1152,1]{2,1,0,3:T(8,128)} fusion(bf16[8,2,128,2048]{3,2,1,0:T(8,128)(2,1)} %bitcast.259, bf16[2,1152,8,128]{1,3,2,0:T(8,128)(2,1)S(1)} %bitcast.250), kind=kOutput, calls=%fused_computation.31 | convolution fusion | flops 9663676416 | bytes 31981568 | tf_op jit(solution)/shard_map/rtcb,tfrc->tbf/dot_general | solution.py:77
  783.0 18.8 %fusion.16 = f32[2,2048,1152,1]{2,1,0,3:T(8,128)} fusion(bf16[8,2,128,2048]{3,2,1,0:T(8,128)(2,1)} %bitcast.256, bf16[2,1152,8,128]{1,3,2,0:T(8,128)(2,1)} %get-tuple-element.39), kind=kOutput, calls=%fused_computation.29 | convolution fusion | flops 9663676416 | bytes 31981568 | tf_op jit(solution)/shard_map/rtcb,tfrc->tbf/dot_general | solution.py:77
  801.8 28.0 %fusion.2 = bf16[2,2048,1152]{2,1,0:T(8,128)(2,1)} fusion(f32[2,2048,1152,1]{2,1,0,3:T(8,128)} %fusion.16, f32[2,2048,1152,1]{2,1,0,3:T(8,128)} %fusion.18, f32[2,2048,1152,1]{2,1,0,3:T(8,128)} %fusion.20, bf16[8,2,128,2048]{3,2,1,0:T(8,128)(2,1)} %bitcast.253, pred[2048,1152]{1,0:T(8,128)(4,1)S(1)} %broadcast_and_fusion, ...), kind=kOutput, calls=%fused_computation.4 | convolution fusion | flops 9687269376 | bytes 81526784 | tf_op jit(solution)/shard_map/rtcb,tfrc->tbf/dot_general | solution.py:77
  829.8 18.5 %fusion.5 = f32[2,8,128,1152]{3,2,1,0:T(8,128)} fusion(bf16[8,2,128,2048]{3,2,1,0:T(8,128)(2,1)} %bitcast.257, bf16[2,2048,1152]{2,1,0:T(8,128)(2,1)} %param.7, pred[2048,1152]{1,0:T(8,128)(4,1)S(1)} %broadcast_and_fusion), kind=kOutput, calls=%fused_computation.10 | convolution fusion | flops 9668395008 | bytes 29622272 | tf_op jit(solution)/shard_map/tbf,rtcb->rtfc/dot_general | solution.py:69
  848.3 2.9 dynamic-slice_bitcast_fusion.3
  852.8 2.4 fusion.24
  855.2 3.3 collective-permute-start.19
  858.5 2.4 fusion.32
  864.7 19.2 %collective-permute-done.12 = bf16[2,2,1152,128]{2,3,0,1:T(8,128)(2,1)S(1)} collective-permute-done((bf16[2,2,1152,128]{2,3,0,1:T(8,128)(2,1)S(1)}, bf16[2,2,1152,128]{2,3,0,1:T(8,128)(2,1)S(1)}, u32[]{:S(2)}, u32[]{:S(2)}) %collective-permute-start.12) | collective-permute-done | bytes 1179680 | tf_op jit(solution)/shard_map/ppermute | solution.py:24
  887.0 22.2 %collective-permute-done.19 = bf16[2,2,1152,128]{2,3,0,1:T(8,128)(2,1)S(1)} collective-permute-done((bf16[2,2,1152,128]{2,3,0,1:T(8,128)(2,1)S(1)}, bf16[2,2,1152,128]{2,3,0,1:T(8,128)(2,1)S(1)}, u32[]{:S(2)}, u32[]{:S(2)}) %collective-permute-start.19) | collective-permute-done | bytes 1179680 | tf_op jit(solution)/shard_map/ppermute | solution.py:24
  910.2 1.9 collective-permute-start.7
  912.1 4.6 fusion.25
  916.7 1.9 collective-permute-start.13
  918.7 15.8 %collective-permute-done.1 = bf16[2,2,1152,128]{2,3,0,1:T(8,128)(2,1)S(1)} collective-permute-done((bf16[2,2,1152,128]{2,3,0,1:T(8,128)(2,1)S(1)}, bf16[2,2,1152,128]{2,3,0,1:T(8,128)(2,1)S(1)}, u32[]{:S(2)}, u32[]{:S(2)}) %collective-permute-start.1) | collective-permute-done | bytes 1179680 | tf_op jit(solution)/shard_map/ppermute | solution.py:24
  937.5 3.7 fusion.37
  942.5 17.4 %collective-permute-done.7 = bf16[2,2,1152,128]{2,3,0,1:T(8,128)(2,1)} collective-permute-done((bf16[2,2,1152,128]{2,3,0,1:T(8,128)(2,1)S(1)}, bf16[2,2,1152,128]{2,3,0,1:T(8,128)(2,1)}, u32[]{:S(2)}, u32[]{:S(2)}) %collective-permute-start.7) | collective-permute-done | bytes 1179680 | tf_op jit(solution)/shard_map/ppermute | solution.py:24
  961.8 3.3 fusion.33
  966.4 18.8 %collective-permute-done.13 = bf16[2,2,1152,128]{2,3,0,1:T(8,128)(2,1)} collective-permute-done((bf16[2,2,1152,128]{2,3,0,1:T(8,128)(2,1)S(1)}, bf16[2,2,1152,128]{2,3,0,1:T(8,128)(2,1)}, u32[]{:S(2)}, u32[]{:S(2)}) %collective-permute-start.13) | collective-permute-done | bytes 1179680 | tf_op jit(solution)/shard_map/ppermute | solution.py:24
  986.4 3.4 fusion.29
  991.1 2.0 fusion.23
  993.0 28.3 %collective-permute-done.10 = bf16[2,2,1152,128]{2,3,0,1:T(8,128)(2,1)S(1)} collective-permute-done((bf16[2,2,1152,128]{2,3,0,1:T(8,128)(2,1)}, bf16[2,2,1152,128]{2,3,0,1:T(8,128)(2,1)S(1)}, u32[]{:S(2)}, u32[]{:S(2)}) %collective-permute-start.10) | collective-permute-done | bytes 1179680 | tf_op jit(solution)/shard_map/ppermute | solution.py:24
  1023.5 3.9 collective-permute-start.8
  1027.8 18.9 %collective-permute-done.16 = bf16[2,2,1152,128]{2,3,0,1:T(8,128)(2,1)S(1)} collective-permute-done((bf16[2,2,1152,128]{2,3,0,1:T(8,128)(2,1)}, bf16[2,2,1152,128]{2,3,0,1:T(8,128)(2,1)S(1)}, u32[]{:S(2)}, u32[]{:S(2)}) %collective-permute-start.16) | collective-permute-done | bytes 1179680 | tf_op jit(solution)/shard_map/ppermute | solution.py:24
  1048.9 3.9 collective-permute-start.14
  1052.8 19.1 %collective-permute-done.23 = bf16[2,2,1152,128]{2,3,0,1:T(8,128)(2,1)S(1)} collective-permute-done((bf16[2,2,1152,128]{2,3,0,1:T(8,128)(2,1)S(1)}, bf16[2,2,1152,128]{2,3,0,1:T(8,128)(2,1)S(1)}, u32[]{:S(2)}, u32[]{:S(2)}) %collective-permute-start.23) | collective-permute-done | bytes 1179680 | tf_op jit(solution)/shard_map/ppermute | solution.py:24
  1071.9 2.1 collective-permute-start.11
  1074.1 2.1 fusion.39
  1076.1 1.9 collective-permute-start.17
  1078.1 19.1 %collective-permute-done.5 = bf16[2,2,1152,128]{2,3,0,1:T(8,128)(2,1)S(1)} collective-permute-done((bf16[2,2,1152,128]{2,3,0,1:T(8,128)(2,1)S(1)}, bf16[2,2,1152,128]{2,3,0,1:T(8,128)(2,1)S(1)}, u32[]{:S(2)}, u32[]{:S(2)}) %collective-permute-start.5) | collective-permute-done | bytes 1179680 | tf_op jit(solution)/shard_map/ppermute | solution.py:24
  1097.2 2.1 fusion.45
  1099.3 23.2 %collective-permute-done.11 = bf16[2,2,1152,128]{2,3,0,1:T(8,128)(2,1)S(1)} collective-permute-done((bf16[2,2,1152,128]{2,3,0,1:T(8,128)(2,1)S(1)}, bf16[2,2,1152,128]{2,3,0,1:T(8,128)(2,1)S(1)}, u32[]{:S(2)}, u32[]{:S(2)}) %collective-permute-start.11) | collective-permute-done | bytes 1179680 | tf_op jit(solution)/shard_map/ppermute | solution.py:24
  1122.9 23.2 %collective-permute-done.17 = bf16[2,2,1152,128]{2,3,0,1:T(8,128)(2,1)S(1)} collective-permute-done((bf16[2,2,1152,128]{2,3,0,1:T(8,128)(2,1)S(1)}, bf16[2,2,1152,128]{2,3,0,1:T(8,128)(2,1)S(1)}, u32[]{:S(2)}, u32[]{:S(2)}) %collective-permute-start.17) | collective-permute-done | bytes 1179680 | tf_op jit(solution)/shard_map/ppermute | solution.py:24
  1146.5 4.1 maximum_bitcast_fusion
  1150.6 11.9 %copy.88 = f32[2,1152,2,4,128]{4,3,2,1,0:T(4,128)} copy(f32[2,1152,2,4,128]{1,4,2,0,3:T(8,128)} %maximum_bitcast_fusion) | data formatting | bytes 18874368 | tf_op jit(solution)/shard_map/transpose | solution.py:83
  1162.4 12.2 %reshape.161 = f32[2,1152,1024]{2,1,0:T(8,128)} reshape(f32[2,1152,2,4,128]{4,3,2,1,0:T(4,128)} %copy.88) | data formatting | bytes 18874368 | tf_op jit(solution)/shard_map/reshape | solution.py:83
  (127 shorter events, 49.2 us)
Async XLA Ops:
  7.2 176.7 %reduce-scatter.9.cloned.1.call-start = ((), (), s32[]{:S(2)}) async-start(), calls=%async_computation.6 | async-start | bytes 18874368 | tf_op jit(solution)/shard_map/reduce_scatter | solution.py:49
  66.6 236.8 %reduce-scatter.11.cloned.1.call-start = ((), (), s32[]{:S(2)}) async-start(), calls=%async_computation.7 | async-start | bytes 18874368 | tf_op jit(solution)/shard_map/reduce_scatter | solution.py:49
  86.3 336.6 %reduce-scatter.7.cloned.1.call-start = ((), (), s32[]{:S(2)}) async-start(), calls=%async_computation.5 | async-start | bytes 18874368 | tf_op jit(solution)/shard_map/reduce_scatter | solution.py:49
  106.9 435.6 %reduce-scatter.5.cloned.1.call-start = ((), (), s32[]{:S(2)}) async-start(), calls=%async_computation.4 | async-start | bytes 18874368 | tf_op jit(solution)/shard_map/reduce_scatter | solution.py:49
  125.2 0.7 copy-start.17
  125.2 0.7 copy-start.19
  125.2 0.7 copy-start.18
  125.3 486.4 %all-gather.15.cloned.1.call-start = ((), (), s32[]{:S(2)}) async-start(), calls=%async_computation.11 | async-start | bytes 9437184 | tf_op jit(solution)/shard_map/all_gather | solution.py:67
  303.4 2.9 copy-start.11
  306.3 2.4 copy-start.10
  542.4 2.9 copy-start.9
  542.4 3.9 copy-start.8
  545.3 2.2 copy-start.5
  545.3 2.4 copy-start.6
  545.3 3.0 copy-start.7
  546.3 2.6 copy-start.2
  546.3 3.2 copy-start.3
  546.4 3.8 copy-start.4
  546.4 4.0 copy-start.12
  556.4 110.7 %all-gather.9.cloned.1.call-start = ((), (), s32[]{:S(2)}) async-start(), calls=%async_computation.8 | async-start | bytes 9437184 | tf_op jit(solution)/shard_map/all_gather | solution.py:67
  557.0 166.4 %all-gather.11.cloned.1.call-start = ((), (), s32[]{:S(2)}) async-start(), calls=%async_computation.9 | async-start | bytes 9437184 | tf_op jit(solution)/shard_map/all_gather | solution.py:67
  557.7 225.3 %all-gather.13.cloned.1.call-start = ((), (), s32[]{:S(2)}) async-start(), calls=%async_computation.10 | async-start | bytes 9437184 | tf_op jit(solution)/shard_map/all_gather | solution.py:67
  558.5 49.6 %copy-start.13 = (bf16[2,128,2048]{2,1,0:T(8,128)(2,1)S(1)}, bf16[2,128,2048]{2,1,0:T(8,128)(2,1)}, u32[]{:S(2)}) copy-start(bf16[2,128,2048]{2,1,0:T(8,128)(2,1)} %get-tuple-element.69) | copy-start | bytes 3145732
  634.2 217.0 %collective-permute-start.18 = (bf16[2,2,1152,128]{2,3,0,1:T(8,128)(2,1)}, bf16[2,2,1152,128]{2,3,0,1:T(8,128)(2,1)}, u32[]{:S(2)}, u32[]{:S(2)}) collective-permute-start(bf16[2,2,1152,128]{2,3,0,1:T(8,128)(2,1)} %get-tuple-element.55), channel_id=1, source_target_pairs={{0,8},{1,9},{2,10},{3,11},{4,12},{5,13},{6,14},{7,15}} | collective-permute-start | bytes 3538952 | tf_op jit(solution)/shard_map/ppermute | solution.py:24
  635.5 250.6 %collective-permute-start.21 = (bf16[2,2,1152,128]{2,3,0,1:T(8,128)(2,1)}, bf16[2,2,1152,128]{2,3,0,1:T(8,128)(2,1)}, u32[]{:S(2)}, u32[]{:S(2)}) collective-permute-start(bf16[2,2,1152,128]{2,3,0,1:T(8,128)(2,1)} %get-tuple-element.56), channel_id=1, source_target_pairs={{24,16},{25,17},{26,18},{27,19},{28,20},{29,21},{30,22},{31,23}} | collective-permute-start | bytes 3538952 | tf_op jit(solution)/shard_map/ppermute | solution.py:24
  689.9 2.8 copy-start
  692.7 168.2 %collective-permute-start = (bf16[2,2,1152,128]{2,3,0,1:T(8,128)(2,1)}, bf16[2,2,1152,128]{2,3,0,1:T(8,128)(2,1)}, u32[]{:S(2)}, u32[]{:S(2)}) collective-permute-start(bf16[2,2,1152,128]{2,3,0,1:T(8,128)(2,1)} %get-tuple-element.43), channel_id=1, source_target_pairs={{0,8},{1,9},{2,10},{3,11},{4,12},{5,13},{6,14},{7,15}} | collective-permute-start | bytes 3538952 | tf_op jit(solution)/shard_map/ppermute | solution.py:24
  694.0 222.7 %collective-permute-start.3 = (bf16[2,2,1152,128]{2,3,0,1:T(8,128)(2,1)}, bf16[2,2,1152,128]{2,3,0,1:T(8,128)(2,1)}, u32[]{:S(2)}, u32[]{:S(2)}) collective-permute-start(bf16[2,2,1152,128]{2,3,0,1:T(8,128)(2,1)} %get-tuple-element.44), channel_id=1, source_target_pairs={{24,16},{25,17},{26,18},{27,19},{28,20},{29,21},{30,22},{31,23}} | collective-permute-start | bytes 3538952 | tf_op jit(solution)/shard_map/ppermute | solution.py:24
  745.5 20.2 %slice-start.5 = ((s8[4718592]{0:T(1024)(128)(4,1)}), s8[4194304]{0:T(1024)(128)(4,1)S(1)}, s32[]{:S(2)}) async-start(s8[4718592]{0:T(1024)(128)(4,1)} %bitcast.249), calls=%async_computation.17 | async-start | bytes 8388608
  745.5 20.2 %slice-start.6 = ((s8[4718592]{0:T(1024)(128)(4,1)}), s8[524288]{0:T(1024)(128)(4,1)S(1)}, s32[]{:S(2)}) async-start(s8[4718592]{0:T(1024)(128)(4,1)} %bitcast.249), calls=%async_computation.18 | async-start | bytes 1048576
  745.5 109.7 %collective-permute-start.6 = (bf16[2,2,1152,128]{2,3,0,1:T(8,128)(2,1)}, bf16[2,2,1152,128]{2,3,0,1:T(8,128)(2,1)}, u32[]{:S(2)}, u32[]{:S(2)}) collective-permute-start(bf16[2,2,1152,128]{2,3,0,1:T(8,128)(2,1)} %get-tuple-element.47), channel_id=1, source_target_pairs={{0,8},{1,9},{2,10},{3,11},{4,12},{5,13},{6,14},{7,15}} | collective-permute-start | bytes 3538952 | tf_op jit(solution)/shard_map/ppermute | solution.py:24
  848.3 37.5 %copy-start.1 = (f32[2,8,128,1152]{3,2,1,0:T(8,128)S(1)}, f32[2,8,128,1152]{3,2,1,0:T(8,128)}, u32[]{:S(2)}) copy-start(f32[2,8,128,1152]{3,2,1,0:T(8,128)} %fusion.5) | copy-start | bytes 28311556
  851.2 32.7 %collective-permute-start.12 = (bf16[2,2,1152,128]{2,3,0,1:T(8,128)(2,1)S(1)}, bf16[2,2,1152,128]{2,3,0,1:T(8,128)(2,1)S(1)}, u32[]{:S(2)}, u32[]{:S(2)}) collective-permute-start(bf16[2,2,1152,128]{2,3,0,1:T(8,128)(2,1)S(1)} %get-tuple-element.51), channel_id=1, source_target_pairs={{0,8},{1,9},{2,10},{3,11},{4,12},{5,13},{6,14},{7,15}} | collective-permute-start | bytes 3538952 | tf_op jit(solution)/shard_map/ppermute | solution.py:24
  852.8 109.0 %slice-start.2 = ((s8[9437184]{0:T(1024)(128)(4,1)}), s8[4194304]{0:T(1024)(128)(4,1)S(1)}, s32[]{:S(2)}) async-start(s8[9437184]{0:T(1024)(128)(4,1)} %bitcast.236), calls=%async_computation.14 | async-start | bytes 8388608
  855.2 54.0 %collective-permute-start.19 = (bf16[2,2,1152,128]{2,3,0,1:T(8,128)(2,1)S(1)}, bf16[2,2,1152,128]{2,3,0,1:T(8,128)(2,1)S(1)}, u32[]{:S(2)}, u32[]{:S(2)}) collective-permute-start(bf16[2,2,1152,128]{2,3,0,1:T(8,128)(2,1)S(1)} %fusion.24), channel_id=1, source_target_pairs={{0,8},{8,16},{1,9},{9,17},{2,10},{10,18},{3,11},{11,19},{4,12},{12... | collective-permute-start | bytes 3538952 | tf_op jit(solution)/shard_map/ppermute | solution.py:24
  858.5 78.9 %slice-start = ((s8[4718592]{0:T(1024)(128)(4,1)}), s8[4194304]{0:T(1024)(128)(4,1)S(1)}, s32[]{:S(2)}) async-start(s8[4718592]{0:T(1024)(128)(4,1)} %bitcast.225), calls=%async_computation.12 | async-start | bytes 8388608
  860.9 100.8 %slice-start.3 = ((s8[9437184]{0:T(1024)(128)(4,1)}), s8[4194304]{0:T(1024)(128)(4,1)S(1)}, s32[]{:S(2)}) async-start(s8[9437184]{0:T(1024)(128)(4,1)} %bitcast.236), calls=%async_computation.15 | async-start | bytes 8388608
  860.9 80.2 %collective-permute-start.9 = (bf16[2,2,1152,128]{2,3,0,1:T(8,128)(2,1)S(1)}, bf16[2,2,1152,128]{2,3,0,1:T(8,128)(2,1)}, u32[]{:S(2)}, u32[]{:S(2)}) collective-permute-start(bf16[2,2,1152,128]{2,3,0,1:T(8,128)(2,1)S(1)} %get-tuple-element.48), channel_id=1, source_target_pairs={{24,16},{25,17},{26,18},{27,19},{28,20},{29,21},{30,22},{31,23}} | collective-permute-start | bytes 3538952 | tf_op jit(solution)/shard_map/ppermute | solution.py:24
  864.7 72.8 %slice-start.1 = ((s8[4718592]{0:T(1024)(128)(4,1)}), s8[524288]{0:T(1024)(128)(4,1)S(1)}, s32[]{:S(2)}) async-start(s8[4718592]{0:T(1024)(128)(4,1)} %bitcast.225), calls=%async_computation.13 | async-start | bytes 1048576
  883.9 50.6 %collective-permute-start.1 = (bf16[2,2,1152,128]{2,3,0,1:T(8,128)(2,1)S(1)}, bf16[2,2,1152,128]{2,3,0,1:T(8,128)(2,1)S(1)}, u32[]{:S(2)}, u32[]{:S(2)}) collective-permute-start(bf16[2,2,1152,128]{2,3,0,1:T(8,128)(2,1)S(1)} %fusion.36), channel_id=1, source_target_pairs={{0,8},{8,16},{1,9},{9,17},{2,10},{10,18},{3,11},{11,19},{4,12},{12... | collective-permute-start | bytes 3538952 | tf_op jit(solution)/shard_map/ppermute | solution.py:24
  886.1 75.7 %slice-start.4 = ((s8[9437184]{0:T(1024)(128)(4,1)}), s8[1048576]{0:T(1024)(128)(4,1)S(1)}, s32[]{:S(2)}) async-start(s8[9437184]{0:T(1024)(128)(4,1)} %bitcast.236), calls=%async_computation.16 | async-start | bytes 2097152
  886.1 79.0 %collective-permute-start.15 = (bf16[2,2,1152,128]{2,3,0,1:T(8,128)(2,1)S(1)}, bf16[2,2,1152,128]{2,3,0,1:T(8,128)(2,1)S(1)}, u32[]{:S(2)}, u32[]{:S(2)}) collective-permute-start(bf16[2,2,1152,128]{2,3,0,1:T(8,128)(2,1)S(1)} %get-tuple-element.52), channel_id=1, source_target_pairs={{24,16},{25,17},{26,18},{27,19},{28,20},{29,21},{30,22},{31,23}} | collective-permute-start | bytes 3538952 | tf_op jit(solution)/shard_map/ppermute | solution.py:24
  909.2 1.0 copy-start.15
  910.2 49.6 %collective-permute-start.7 = (bf16[2,2,1152,128]{2,3,0,1:T(8,128)(2,1)S(1)}, bf16[2,2,1152,128]{2,3,0,1:T(8,128)(2,1)}, u32[]{:S(2)}, u32[]{:S(2)}) collective-permute-start(bf16[2,2,1152,128]{2,3,0,1:T(8,128)(2,1)S(1)} %fusion.32), channel_id=1, source_target_pairs={{0,8},{8,16},{1,9},{9,17},{2,10},{10,18},{3,11},{11,19},{4,12},{12... | collective-permute-start | bytes 3538952 | tf_op jit(solution)/shard_map/ppermute | solution.py:24
  916.7 68.4 %collective-permute-start.13 = (bf16[2,2,1152,128]{2,3,0,1:T(8,128)(2,1)S(1)}, bf16[2,2,1152,128]{2,3,0,1:T(8,128)(2,1)}, u32[]{:S(2)}, u32[]{:S(2)}) collective-permute-start(bf16[2,2,1152,128]{2,3,0,1:T(8,128)(2,1)S(1)} %fusion.28), channel_id=1, source_target_pairs={{0,8},{8,16},{1,9},{9,17},{2,10},{10,18},{3,11},{11,19},{4,12},{12... | collective-permute-start | bytes 3538952 | tf_op jit(solution)/shard_map/ppermute | solution.py:24
  934.5 1.1 copy-start.16
  935.5 113.4 %collective-permute-start.20 = (bf16[2,2,1152,128]{2,3,0,1:T(8,128)(2,1)S(1)}, bf16[2,2,1152,128]{2,3,0,1:T(8,128)(2,1)S(1)}, u32[]{:S(2)}, u32[]{:S(2)}) collective-permute-start(bf16[2,2,1152,128]{2,3,0,1:T(8,128)(2,1)S(1)} %get-tuple-element.53), channel_id=1, source_target_pairs={{0,8},{8,16},{16,24},{1,9},{9,17},{17,25},{2,10},{10,18},{18,26},{... | collective-permute-start | bytes 3538952 | tf_op jit(solution)/shard_map/ppermute | solution.py:24
  941.2 48.6 %collective-permute-start.22 = (bf16[2,2,1152,128]{2,3,0,1:T(8,128)(2,1)}, bf16[2,2,1152,128]{2,3,0,1:T(8,128)(2,1)S(1)}, u32[]{:S(2)}, u32[]{:S(2)}) collective-permute-start(bf16[2,2,1152,128]{2,3,0,1:T(8,128)(2,1)} %get-tuple-element.54), channel_id=1, source_target_pairs={{24,16},{16,8},{25,17},{17,9},{26,18},{18,10},{27,19},{19,11},{28,... | collective-permute-start | bytes 3538952 | tf_op jit(solution)/shard_map/ppermute | solution.py:24
  959.9 116.3 %collective-permute-start.2 = (bf16[2,2,1152,128]{2,3,0,1:T(8,128)(2,1)}, bf16[2,2,1152,128]{2,3,0,1:T(8,128)(2,1)S(1)}, u32[]{:S(2)}, u32[]{:S(2)}) collective-permute-start(bf16[2,2,1152,128]{2,3,0,1:T(8,128)(2,1)} %get-tuple-element.41), channel_id=1, source_target_pairs={{0,8},{8,16},{16,24},{1,9},{9,17},{17,25},{2,10},{10,18},{18,26},{... | collective-permute-start | bytes 3538952 | tf_op jit(solution)/shard_map/ppermute | solution.py:24
  965.1 58.4 %collective-permute-start.4 = (bf16[2,2,1152,128]{2,3,0,1:T(8,128)(2,1)}, bf16[2,2,1152,128]{2,3,0,1:T(8,128)(2,1)S(1)}, u32[]{:S(2)}, u32[]{:S(2)}) collective-permute-start(bf16[2,2,1152,128]{2,3,0,1:T(8,128)(2,1)} %get-tuple-element.42), channel_id=1, source_target_pairs={{24,16},{16,8},{25,17},{17,9},{26,18},{18,10},{27,19},{19,11},{28,... | collective-permute-start | bytes 3538952 | tf_op jit(solution)/shard_map/ppermute | solution.py:24
  985.1 36.2 %collective-permute-start.10 = (bf16[2,2,1152,128]{2,3,0,1:T(8,128)(2,1)}, bf16[2,2,1152,128]{2,3,0,1:T(8,128)(2,1)S(1)}, u32[]{:S(2)}, u32[]{:S(2)}) collective-permute-start(bf16[2,2,1152,128]{2,3,0,1:T(8,128)(2,1)} %get-tuple-element.46), channel_id=1, source_target_pairs={{24,16},{16,8},{25,17},{17,9},{26,18},{18,10},{27,19},{19,11},{28,... | collective-permute-start | bytes 3538952 | tf_op jit(solution)/shard_map/ppermute | solution.py:24
  989.8 56.9 %collective-permute-start.16 = (bf16[2,2,1152,128]{2,3,0,1:T(8,128)(2,1)}, bf16[2,2,1152,128]{2,3,0,1:T(8,128)(2,1)S(1)}, u32[]{:S(2)}, u32[]{:S(2)}) collective-permute-start(bf16[2,2,1152,128]{2,3,0,1:T(8,128)(2,1)} %get-tuple-element.50), channel_id=1, source_target_pairs={{24,16},{16,8},{25,17},{17,9},{26,18},{18,10},{27,19},{19,11},{28,... | collective-permute-start | bytes 3538952 | tf_op jit(solution)/shard_map/ppermute | solution.py:24
  1021.4 50.6 %collective-permute-start.23 = (bf16[2,2,1152,128]{2,3,0,1:T(8,128)(2,1)S(1)}, bf16[2,2,1152,128]{2,3,0,1:T(8,128)(2,1)S(1)}, u32[]{:S(2)}, u32[]{:S(2)}) collective-permute-start(bf16[2,2,1152,128]{2,3,0,1:T(8,128)(2,1)S(1)} %fusion.23), channel_id=1, source_target_pairs={{24,16},{16,8},{8,0},{25,17},{17,9},{9,1},{26,18},{18,10},{10,2},{... | collective-permute-start | bytes 3538952 | tf_op jit(solution)/shard_map/ppermute | solution.py:24
  1023.5 75.7 %collective-permute-start.8 = (bf16[2,2,1152,128]{2,3,0,1:T(8,128)(2,1)S(1)}, bf16[2,2,1152,128]{2,3,0,1:T(8,128)(2,1)S(1)}, u32[]{:S(2)}, u32[]{:S(2)}) collective-permute-start(bf16[2,2,1152,128]{2,3,0,1:T(8,128)(2,1)S(1)} %get-tuple-element.45), channel_id=1, source_target_pairs={{0,8},{8,16},{16,24},{1,9},{9,17},{17,25},{2,10},{10,18},{18,26},{... | collective-permute-start | bytes 3538952 | tf_op jit(solution)/shard_map/ppermute | solution.py:24
  1027.8 21.1 %copy-start.14 = (bf16[2,2,1152,128]{2,3,0,1:T(8,128)(2,1)S(1)}, bf16[2,2,1152,128]{2,3,0,1:T(8,128)(2,1)}, u32[]{:S(2)}) copy-start(bf16[2,2,1152,128]{2,3,0,1:T(8,128)(2,1)} %get-tuple-element.49) | copy-start | bytes 3538948
  1046.6 50.6 %collective-permute-start.5 = (bf16[2,2,1152,128]{2,3,0,1:T(8,128)(2,1)S(1)}, bf16[2,2,1152,128]{2,3,0,1:T(8,128)(2,1)S(1)}, u32[]{:S(2)}, u32[]{:S(2)}) collective-permute-start(bf16[2,2,1152,128]{2,3,0,1:T(8,128)(2,1)S(1)} %fusion.35), channel_id=1, source_target_pairs={{24,16},{16,8},{8,0},{25,17},{17,9},{9,1},{26,18},{18,10},{10,2},{... | collective-permute-start | bytes 3538952 | tf_op jit(solution)/shard_map/ppermute | solution.py:24
  1048.9 74.0 %collective-permute-start.14 = (bf16[2,2,1152,128]{2,3,0,1:T(8,128)(2,1)S(1)}, bf16[2,2,1152,128]{2,3,0,1:T(8,128)(2,1)S(1)}, u32[]{:S(2)}, u32[]{:S(2)}) collective-permute-start(bf16[2,2,1152,128]{2,3,0,1:T(8,128)(2,1)S(1)} %copy-done.14), channel_id=1, source_target_pairs={{0,8},{8,16},{16,24},{1,9},{9,17},{17,25},{2,10},{10,18},{18,26},{... | collective-permute-start | bytes 3538952 | tf_op jit(solution)/shard_map/ppermute | solution.py:24
  1071.9 50.6 %collective-permute-start.11 = (bf16[2,2,1152,128]{2,3,0,1:T(8,128)(2,1)S(1)}, bf16[2,2,1152,128]{2,3,0,1:T(8,128)(2,1)S(1)}, u32[]{:S(2)}, u32[]{:S(2)}) collective-permute-start(bf16[2,2,1152,128]{2,3,0,1:T(8,128)(2,1)S(1)} %fusion.31), channel_id=1, source_target_pairs={{24,16},{16,8},{8,0},{25,17},{17,9},{9,1},{26,18},{18,10},{10,2},{... | collective-permute-start | bytes 3538952 | tf_op jit(solution)/shard_map/ppermute | solution.py:24
  1076.1 69.9 %collective-permute-start.17 = (bf16[2,2,1152,128]{2,3,0,1:T(8,128)(2,1)S(1)}, bf16[2,2,1152,128]{2,3,0,1:T(8,128)(2,1)S(1)}, u32[]{:S(2)}, u32[]{:S(2)}) collective-permute-start(bf16[2,2,1152,128]{2,3,0,1:T(8,128)(2,1)S(1)} %fusion.27), channel_id=1, source_target_pairs={{24,16},{16,8},{8,0},{25,17},{17,9},{9,1},{26,18},{18,10},{10,2},{... | collective-permute-start | bytes 3538952 | tf_op jit(solution)/shard_map/ppermute | solution.py:24
Sparse Core Ops, SparseCore 0:
  66.8 117.1 reduce-scatter.8
  187.5 115.9 reduce-scatter.10
  307.0 115.9 reduce-scatter.6
  426.4 115.9 reduce-scatter.4
  556.5 54.4 all-gather.14
  612.7 54.3 all-gather.8
  669.0 54.3 all-gather.10
  725.3 54.3 all-gather.12
